TPU v7x, 32 devices: a whole 2x2x4 slice. The times are simulated.
32 devices in a mesh: seq: 8 (over z, y), head: 4 (over x, core).
Axes of the slice: x: 2, y: 2, z: 4, core: 2. Of those that a mesh axis runs over, the one named last changes fastest.
Arguments:
- query: bfloat16 [4096, 8192], P('seq', 'head'), may hold values from -1.5 to 1.5
- key_in: bfloat16 [4096, 8192], P('seq', 'head'), may hold values from -0.5 to 0.5
- value: bfloat16 [4096, 8192], P('seq', 'head'), may hold values from -6 to 6
- gate: bfloat16 [4096, 8192], P(('seq', 'head')), may hold values from -6 to 6
- gain: float32 [8192], replicated, may hold values from 0.5 to 1.5
- grad_out: bfloat16 [4096, 8192], P(('seq', 'head')), may hold values from -6 to 6
Outputs:
- grad_query: bfloat16 [4096, 8192], P('seq', 'head')
- grad_key: bfloat16 [4096, 8192], P('seq', 'head')
- grad_value: bfloat16 [4096, 8192], P('seq', 'head')
- grad_gate: bfloat16 [4096, 8192], P(('seq', 'head'))
All inputs are finite; a program needn't handle non-finite values.
Results may differ from a plain program's by a relative error of at most 0.012.
Values may be sent and summed in bfloat16 or wider, within the bound.
A program may use at most 128 MiB of HBM per device.

v0:
```python
import jax
import jax.numpy as jnp
from jax import lax
from jax.sharding import PartitionSpec as P

HEAD_DIM = 128


def carried_in(value, axis, combine, identity):
    peers, place = (lax.axis_size(axis), lax.axis_index(axis))
    everything = lax.all_gather(value.astype(jnp.bfloat16), axis)
    start = jnp.broadcast_to(jnp.asarray(identity, value.dtype), value.shape)

    def step(k, before):
        at = peers - 1 - k
        reached = at > place
        new = combine(before, everything[at].astype(value.dtype))
        return jnp.where(reached, new, before)

    return lax.fori_loop(0, peers, step, start)


def add_states(earlier, later_part):
    return earlier + later_part


def split_heads(matrix, head_dim):
    return matrix.reshape(matrix.shape[0], matrix.shape[1] // head_dim, head_dim)


def on_device(query, key_in, value, gate, gain, grad_out):
    head_dim = HEAD_DIM
    tok_here = query.shape[0]
    queries = split_heads(query, head_dim)
    keys_here = split_heads(key_in, head_dim)
    values_here = split_heads(value, head_dim)
    local_state = jnp.einsum(
        "thd,the->hde", keys_here, values_here, preferred_element_type=jnp.float32
    )
    zero_state = jnp.zeros_like(local_state)
    my_index = lax.axis_index("seq")
    shard_piece = lax.all_gather(
        local_state[None].astype(jnp.bfloat16), "seq", axis=0, tiled=True
    ).astype(jnp.float32)
    position = jnp.arange(shard_piece.shape[0], dtype=jnp.int32)
    keep_rows = (position < my_index).astype(jnp.float32)
    prefix = zero_state + jnp.sum(keep_rows[:, None, None, None] * shard_piece, axis=0)
    causal = jnp.tril(jnp.ones((tok_here, tok_here), dtype=bool))
    scores = jnp.einsum("thd,shd->hts", queries, keys_here, preferred_element_type=jnp.float32)
    masked_scores = jnp.where(causal[None], scores, 0.0).astype(jnp.bfloat16)
    prefix_low = prefix.astype(jnp.bfloat16)
    attn_out = jnp.einsum(
        "hts,she->the", masked_scores, values_here, preferred_element_type=jnp.float32
    )
    attn_out = attn_out + jnp.einsum(
        "thd,hde->the", queries, prefix_low, preferred_element_type=jnp.float32
    )
    attn_out = attn_out.astype(jnp.bfloat16).reshape(tok_here, -1)
    token_rows = lax.all_to_all(attn_out, "head", split_axis=0, concat_axis=1, tiled=True)
    rows_wide = token_rows.astype(jnp.float32)
    inv_rms = lax.rsqrt(jnp.mean(rows_wide * rows_wide, axis=1, keepdims=True) + 1e-06)
    normed = rows_wide * inv_rms
    gate_wide = gate.astype(jnp.float32)
    sigmoid_gate = jax.nn.sigmoid(gate_wide)
    scaled = grad_out.astype(jnp.float32) * gain[None, :]
    grad_gate = (scaled * normed * sigmoid_gate * (1.0 + gate_wide * (1.0 - sigmoid_gate))).astype(
        jnp.bfloat16
    )
    weighted = scaled * gate_wide * sigmoid_gate
    grad_rows = inv_rms * (weighted - normed * jnp.mean(weighted * normed, axis=1, keepdims=True))
    grad_rows = grad_rows.astype(jnp.bfloat16)
    grad_heads = lax.all_to_all(grad_rows, "head", split_axis=1, concat_axis=0, tiled=True)
    grad_attn = split_heads(grad_heads, head_dim)
    local_grad = jnp.einsum("thd,the->hde", queries, grad_attn, preferred_element_type=jnp.float32)
    suffix = carried_in(local_grad, "seq", add_states, zero_state)
    suffix_low = suffix.astype(jnp.bfloat16)
    grad_scores = jnp.einsum(
        "the,she->hts", grad_attn, values_here, preferred_element_type=jnp.float32
    )
    grad_scores = jnp.where(causal[None], grad_scores, 0.0).astype(jnp.bfloat16)
    grad_query = jnp.einsum(
        "hts,shd->thd", grad_scores, keys_here, preferred_element_type=jnp.float32
    )
    grad_query = grad_query + jnp.einsum(
        "the,hde->thd", grad_attn, prefix_low, preferred_element_type=jnp.float32
    )
    grad_key = jnp.einsum("hts,thd->shd", grad_scores, queries, preferred_element_type=jnp.float32)
    grad_key = grad_key + jnp.einsum(
        "she,hde->shd", values_here, suffix_low, preferred_element_type=jnp.float32
    )
    grad_value = jnp.einsum(
        "hts,the->she", masked_scores, grad_attn, preferred_element_type=jnp.float32
    )
    grad_value = grad_value + jnp.einsum(
        "shd,hde->she", keys_here, suffix_low, preferred_element_type=jnp.float32
    )
    return (
        grad_query.astype(jnp.bfloat16).reshape(tok_here, -1),
        grad_key.astype(jnp.bfloat16).reshape(tok_here, -1),
        grad_value.astype(jnp.bfloat16).reshape(tok_here, -1),
        grad_gate,
    )


def solution(mesh):
    in_specs = (
        P("seq", "head"),
        P("seq", "head"),
        P("seq", "head"),
        P(("seq", "head"), None),
        P(),
        P(("seq", "head"), None),
    )
    out_specs = (P("seq", "head"), P("seq", "head"), P("seq", "head"), P(("seq", "head"), None))
    return jax.shard_map(
        on_device, mesh=mesh, in_specs=in_specs, out_specs=out_specs, check_vma=False
    )
```

profile of v0, /device:TPU:0, one launch (start us, length us, event | category | flops | bytes accessed | tf_op | source)
XLA Modules:
  0.0 316.0 jit_solution(6141891403211392233)
XLA Ops:
  7.2 0.0 copy-start
  7.2 0.0 all-gather.5.cloned.1.call-start
  7.2 3.7 %copy.120 = bf16[64,8,16,128]{3,2,1,0:T(8,128)(2,1)} copy(bf16[64,8,16,128]{3,1,2,0:T(8,128)(2,1)} %bitcast.129) | data formatting | bytes 4194304
  10.9 4.3 %copy.88 = bf16[512,16,128]{0,2,1:T(8,128)(2,1)} copy(bf16[512,16,128]{2,1,0:T(8,128)(2,1)} %bitcast.128) | data formatting | bytes 4194304 | tf_op jit(solution)/shard_map/reshape | solution.py:28
  15.2 0.0 copy-done
  15.2 3.1 fusion.39
  18.3 0.0 all-gather.5.cloned.1.call-update
  18.3 0.1 iota_compare_fusion
  18.4 4.6 %select_convert_fusion.1 = bf16[16,512,512]{2,1,0:T(8,128)(2,1)S(1)} fusion(pred[512,512]{1,0:T(8,128)(4,1)S(1)} %iota_compare_fusion, bf16[512,2048]{1,0:T(8,128)(2,1)} %param.9, bf16[512,2048]{1,0:T(8,128)(2,1)} %param.8), kind=kOutput, calls=%fused_computation.2 | convolution fusion | flops 1082130432 | bytes 12845056 | tf_op jit(solution)/shard_map/thd,shd->hts/dot_general | solution.py:49
  23.0 0.0 copy-start.1
  23.1 3.2 %copy-done.1 = bf16[16,512,512]{2,1,0:T(8,128)(2,1)} copy-done((bf16[16,512,512]{2,1,0:T(8,128)(2,1)}, bf16[16,512,512]{2,1,0:T(8,128)(2,1)S(1)}, u32[]{:S(2)}) %copy-start.1) | copy-done | bytes 8388632
  26.3 4.3 %fusion.17 = f32[16,512,128]{2,1,0:T(8,128)} fusion(bf16[16,512,512]{2,1,0:T(8,128)(2,1)S(1)} %select_convert_fusion.1, bf16[512,2048]{1,0:T(8,128)(2,1)S(1)} %copy-done), kind=kOutput, calls=%fused_computation.34 | convolution fusion | flops 1073741824 | bytes 14680064 | tf_op jit(solution)/shard_map/hts,she->the/dot_general | solution.py:52
  30.6 63.4 %all-gather.5.cloned.1.call-done = bf16[128,128,128]{2,1,0:T(8,128)(2,1)} async-done(((bf16[16,128,128]{2,1,0:T(8,128)(2,1)}), bf16[128,128,128]{2,1,0:T(8,128)(2,1)}) %all-gather.5.cloned.1.call-update) | async-done | bytes 4194320 | tf_op jit(solution)/shard_map/all_gather | solution.py:42
  94.0 3.3 %fusion = bf16[16,128,128]{2,1,0:T(8,128)(2,1)S(1)} fusion(bf16[8,16,128,128]{3,2,1,0:T(8,128)(2,1)} %bitcast.132, f32[8]{0:T(128)S(1)} %compare_convert_fusion), kind=kLoop, calls=%fused_computation.4 | loop fusion | flops 6029312 | bytes 4718624 | tf_op jit(solution)/shard_map/reduce_sum | solution.py:47
  97.3 0.2 copy-done.8
  97.4 2.5 fusion.11
  99.9 2.7 copy.93
  102.6 4.2 %all_to_all.22 = bf16[4,128,2048]{2,1,0:T(8,128)(2,1)} reshape(bf16[512,16,128]{2,1,0:T(8,128)(2,1)} %copy.93) | data formatting | bytes 4194304 | tf_op jit(solution)/shard_map/all_to_all | solution.py:59
  106.8 4.5 %all-to-all-start = ((bf16[4,128,2048]{2,1,0:T(8,128)(2,1)}), bf16[4,128,2048]{2,1,0:T(8,128)(2,1)}, u32[]{:S(2)}, u32[]{:S(2)}) async-start(bf16[4,128,2048]{2,1,0:T(8,128)(2,1)} %all_to_all.22), calls=%async_computation | async-start | bytes 4194304 | tf_op jit(solution)/shard_map/all_to_all | solution.py:59
  111.2 0.2 all-gather.7.cloned.1.call-start
  111.5 4.1 %copy.95 = bf16[128,8192]{0,1:T(8,128)(2,1)} copy(bf16[128,8192]{1,0:T(8,128)(2,1)} %param.11) | data formatting | bytes 4194304 | tf_op args[3]
  115.5 4.1 %copy.94 = bf16[128,8192]{0,1:T(8,128)(2,1)} copy(bf16[128,8192]{1,0:T(8,128)(2,1)} %param.13) | data formatting | bytes 4194304 | tf_op args[5]
  119.6 17.4 %all-to-all-done = bf16[4,128,2048]{2,1,0:T(8,128)(2,1)} async-done(((bf16[4,128,2048]{2,1,0:T(8,128)(2,1)}), bf16[4,128,2048]{2,1,0:T(8,128)(2,1)}, u32[]{:S(2)}, u32[]{:S(2)}) %all-to-all-start) | async-done | bytes 2097184 | tf_op jit(solution)/shard_map/all_to_all | solution.py:59
  137.0 2.1 fusion.1
  139.0 4.1 %convert_bitcast_fusion = f32[128,4,2048]{2,0,1:T(8,128)} fusion(bf16[4,128,2048]{2,1,0:T(8,128)(2,1)} %all-to-all-done), kind=kLoop, calls=%fused_computation.8 | loop fusion | flops 1048576 | bytes 6291456 | tf_op jit(solution)/shard_map/convert_element_type | solution.py:60
  143.1 5.4 %copy.96 = f32[128,4,2048]{0,2,1:T(8,128)} copy(f32[128,4,2048]{2,0,1:T(8,128)} %convert_bitcast_fusion) | data formatting | bytes 8388608 | tf_op jit(solution)/shard_map/convert_element_type | solution.py:60
  148.5 0.0 copy-start.7
  148.5 6.7 %multiply_reduce_fusion = f32[128]{0:T(128)S(1)} fusion(f32[128,4,2048]{0,2,1:T(8,128)} %copy.96, f32[128]{0:T(128)S(1)} %add_rsqrt_fusion, bf16[128,8192]{0,1:T(8,128)(2,1)} %copy.95, f32[8192]{0:T(1024)S(1)} %copy-done.12, bf16[128,8192]{0,1:T(8,128)(2,1)} %copy.94), kind=kLoop, calls=%fused_computation.27 | loop fusion | flops 11534208 | bytes 8422400 | tf_op jit(solution)/shard_map/reduce_sum | solution.py:70
  155.3 4.4 %fusion.8 = (bf16[128,8192]{0,1:T(8,128)(2,1)}, bf16[128,8192]{0,1:T(8,128)(2,1)}) fusion(bf16[128,8192]{0,1:T(8,128)(2,1)S(1)} %copy-done.6, bf16[128,8192]{0,1:T(8,128)(2,1)S(1)} %copy-done.7, f32[128,4,2048]{0,2,1:T(8,128)S(1)} %copy-done.2, f32[8192]{0:T(1024)S(1)} %copy-done.12, f32[128]{0:T(128)S(1)} %add_rsqrt_fusion, f32[128]{0:T(128)S(1)} %broadcast_multiply_fusion), kind=kLoop, calls=%fused_computation.17 | loop fusion | flops 20971520 | bytes 12616704 | tf_op jit(solution)/shard_map/convert_element_type | solution.py:66
  159.7 3.9 %copy.97 = bf16[128,4,2048]{2,0,1:T(8,128)(2,1)} copy(bf16[128,4,2048]{0,2,1:T(8,128)(2,1)} %bitcast.124) | data formatting | bytes 4194304 | tf_op jit(solution)/shard_map/all_to_all | solution.py:72
  163.7 29.2 %all_to_all.29 = bf16[128,4,2048]{2,0,1:T(8,128)(2,1)S(1)} all-to-all(bf16[128,4,2048]{2,0,1:T(8,128)(2,1)} %copy.97), channel_id=1, replica_groups=mesh['seq'=8,'head'=4] {'head'}, dimensions={1} | all-to-all | bytes 4194304 | tf_op jit(solution)/shard_map/all_to_all | solution.py:72
  192.9 2.0 copy.121
  194.9 4.3 %copy.103 = bf16[512,16,128]{0,2,1:T(8,128)(2,1)} copy(bf16[512,16,128]{2,1,0:T(8,128)(2,1)} %bitcast.127) | data formatting | bytes 4194304 | tf_op jit(solution)/shard_map/reshape | solution.py:28
  199.2 2.9 fusion.42
  202.1 1.0 copy.105
  203.2 0.0 all-gather.7.cloned.1.call-update
  203.2 4.1 %copy.113 = bf16[128,8192]{1,0:T(8,128)(2,1)} copy(bf16[128,8192]{0,1:T(8,128)(2,1)} %get-tuple-element.166) | data formatting | bytes 4194304
  207.3 4.4 %select_convert_fusion = bf16[16,512,512]{2,1,0:T(8,128)(2,1)S(1)} fusion(bf16[512,16,128]{0,2,1:T(8,128)(2,1)} %copy.103, pred[512,512]{1,0:T(8,128)(4,1)S(1)} %iota_compare_fusion, bf16[512,2048]{1,0:T(8,128)(2,1)S(1)} %copy-done), kind=kOutput, calls=%fused_computation.1 | convolution fusion | flops 1082130432 | bytes 12845056 | tf_op jit(solution)/shard_map/the,she->hts/dot_general | solution.py:77
  211.7 0.0 copy-done.9
  211.7 0.0 copy-start.3
  211.7 0.0 copy-start.5
  211.7 4.8 %fusion.49 = f32[16,512,128]{1,2,0:T(8,128)} fusion(bf16[16,512,512]{2,1,0:T(8,128)(2,1)S(1)} %select_convert_fusion, bf16[512,16,128]{0,2,1:T(8,128)(2,1)S(1)} %copy-done.9), kind=kOutput, calls=%fused_computation.64 | convolution fusion | flops 1073741824 | bytes 14680064 | tf_op jit(solution)/shard_map/hts,shd->thd/dot_general | solution.py:81
  216.5 0.0 copy-done.3
  216.5 4.5 %fusion.10 = bf16[512,16,128]{0,2,1:T(8,128)(2,1)} fusion(f32[16,512,128]{1,2,0:T(8,128)} %fusion.49, bf16[512,16,128]{0,2,1:T(8,128)(2,1)S(1)} %copy-done.5, bf16[16,128,128]{2,1,0:T(8,128)(2,1)} %copy-done.11), kind=kOutput, calls=%fused_computation.21 | convolution fusion | flops 270532608 | bytes 8912896 | tf_op jit(solution)/shard_map/the,hde->thd/dot_general | solution.py:84
  221.0 3.9 %copy.110 = bf16[512,2048]{1,0:T(8,128)(2,1)} copy(bf16[512,2048]{0,1:T(8,128)(2,1)} %bitcast.125) | data formatting | bytes 4194304
  224.9 7.3 %fusion.50 = f32[16,128,512]{2,1,0:T(8,128)} fusion(bf16[512,16,128]{0,2,1:T(8,128)(2,1)} %copy.103, bf16[16,512,512]{2,1,0:T(8,128)(2,1)} %copy-done.1), kind=kOutput, calls=%fused_computation.65 | convolution fusion | flops 1073741824 | bytes 14680064 | tf_op jit(solution)/shard_map/hts,the->she/dot_general | solution.py:91
  232.2 41.6 %all-gather.7.cloned.1.call-done = bf16[128,128,128]{2,1,0:T(8,128)(2,1)} async-done(((bf16[16,128,128]{2,1,0:T(8,128)(2,1)}), bf16[128,128,128]{2,1,0:T(8,128)(2,1)}) %all-gather.7.cloned.1.call-update) | async-done | bytes 4194320 | tf_op jit(solution)/shard_map/all_gather | solution.py:11
  273.8 13.1 %while.16 = (s32[]{:T(128)}, f32[16,128,128]{2,1,0:T(8,128)S(1)}, s32[]{:T(128)}, bf16[8,16,128,128]{3,2,1,0:T(8,128)(2,1)}, s32[]{:T(128)}, /*index=5*/s32[]{:T(128)}, s32[]{:T(128)}, s32[]{:T(128)}) while((s32[]{:T(128)}, f32[16,128,128]{2,1,0:T(8,128)S(1)}, s32[]{:T(128)}, bf16[8,16,128,128]{3,2,1,0:T(8,128)(2,1)}, s32[]{:T(128)}, ...), condition=%wide.region_4.5_spmd.clone, body=%wide.region_3.4_spmd.clone.sunk | while | flops 1048584 | bytes 2621603 | solution.py:20
  273.8 1.6 add_select_fusion.2
  275.4 1.6 add_select_fusion.2
  277.0 1.6 add_select_fusion.2
  278.7 1.6 add_select_fusion.2
  280.3 1.6 add_select_fusion.2
  282.0 1.6 add_select_fusion.2
  283.6 1.6 add_select_fusion.2
  285.3 1.6 add_select_fusion.2
  286.9 0.0 copy-start.10
  286.9 2.9 fusion.12
  289.8 0.6 copy-done.4
  290.3 0.9 copy-done.10
  291.3 2.2 add_convert_fusion
  293.4 3.9 %copy.112 = bf16[512,2048]{1,0:T(8,128)(2,1)} copy(bf16[512,2048]{0,1:T(8,128)(2,1)} %bitcast.130) | data formatting | bytes 4194304
  297.3 7.9 %fusion.9 = bf16[512,16,128]{0,2,1:T(8,128)(2,1)} fusion(f32[16,128,512]{2,1,0:T(8,128)} %fusion.12, bf16[16,512,512]{2,1,0:T(8,128)(2,1)} %copy-done.3, bf16[512,2048]{1,0:T(8,128)(2,1)} %param.8), kind=kOutput, calls=%fused_computation.19 | convolution fusion | flops 1075838976 | bytes 16777216 | tf_op jit(solution)/shard_map/hts,thd->shd/dot_general | solution.py:87
  305.3 3.9 %copy.111 = bf16[512,2048]{1,0:T(8,128)(2,1)} copy(bf16[512,2048]{0,1:T(8,128)(2,1)} %bitcast.131) | data formatting | bytes 4194304
  (17 shorter events, 0.0 us)
Async XLA Ops:
  7.2 8.0 %copy-start = (bf16[512,2048]{1,0:T(8,128)(2,1)S(1)}, bf16[512,2048]{1,0:T(8,128)(2,1)}, u32[]{:S(2)}) copy-start(bf16[512,2048]{1,0:T(8,128)(2,1)} %param.10) | copy-start | bytes 6291460
  7.2 86.8 %all-gather.5.cloned.1.call-start = ((), (), s32[]{:S(2)}) async-start(), calls=%async_computation.2 | async-start | bytes 4718592 | tf_op jit(solution)/shard_map/all_gather | solution.py:42
  23.0 3.2 %copy-start.1 = (bf16[16,512,512]{2,1,0:T(8,128)(2,1)}, bf16[16,512,512]{2,1,0:T(8,128)(2,1)S(1)}, u32[]{:S(2)}) copy-start(bf16[16,512,512]{2,1,0:T(8,128)(2,1)S(1)} %select_convert_fusion.1) | copy-start | bytes 25165828
  94.0 3.4 %copy-start.8 = (f32[16,512,128]{2,1,0:T(8,128)S(1)}, f32[16,512,128]{2,1,0:T(8,128)}, u32[]{:S(2)}) copy-start(f32[16,512,128]{2,1,0:T(8,128)} %fusion.17) | copy-start | bytes 12582916
  97.4 2.5 copy-start.11
  106.8 30.2 %all-to-all-start = ((bf16[4,128,2048]{2,1,0:T(8,128)(2,1)}), bf16[4,128,2048]{2,1,0:T(8,128)(2,1)}, u32[]{:S(2)}, u32[]{:S(2)}) async-start(bf16[4,128,2048]{2,1,0:T(8,128)(2,1)} %all_to_all.22), calls=%async_computation | async-start | bytes 4194304 | tf_op jit(solution)/shard_map/all_to_all | solution.py:59
  111.2 162.5 %all-gather.7.cloned.1.call-start = ((), (), s32[]{:S(2)}) async-start(), calls=%async_computation.3 | async-start | bytes 4718592 | tf_op jit(solution)/shard_map/all_gather | solution.py:11
  143.1 5.4 %copy-start.12 = (f32[8192]{0:T(1024)S(1)}, f32[8192]{0:T(1024)}, u32[]{:S(2)}) copy-start(f32[8192]{0:T(1024)} %param.12) | copy-start | bytes 98308
  148.5 6.8 %copy-start.2 = (f32[128,4,2048]{0,2,1:T(8,128)S(1)}, f32[128,4,2048]{0,2,1:T(8,128)}, u32[]{:S(2)}) copy-start(f32[128,4,2048]{0,2,1:T(8,128)} %copy.96) | copy-start | bytes 12582916
  148.5 6.8 %copy-start.6 = (bf16[128,8192]{0,1:T(8,128)(2,1)S(1)}, bf16[128,8192]{0,1:T(8,128)(2,1)}, u32[]{:S(2)}) copy-start(bf16[128,8192]{0,1:T(8,128)(2,1)} %copy.95) | copy-start | bytes 6291460
  148.5 6.8 %copy-start.7 = (bf16[128,8192]{0,1:T(8,128)(2,1)S(1)}, bf16[128,8192]{0,1:T(8,128)(2,1)}, u32[]{:S(2)}) copy-start(bf16[128,8192]{0,1:T(8,128)(2,1)} %copy.94) | copy-start | bytes 6291460
  207.3 4.4 %copy-start.9 = (bf16[512,16,128]{0,2,1:T(8,128)(2,1)S(1)}, bf16[512,16,128]{0,2,1:T(8,128)(2,1)}, u32[]{:S(2)}) copy-start(bf16[512,16,128]{0,2,1:T(8,128)(2,1)} %copy.88) | copy-start | bytes 6291460
  211.7 4.8 %copy-start.3 = (bf16[16,512,512]{2,1,0:T(8,128)(2,1)}, bf16[16,512,512]{2,1,0:T(8,128)(2,1)S(1)}, u32[]{:S(2)}) copy-start(bf16[16,512,512]{2,1,0:T(8,128)(2,1)S(1)} %select_convert_fusion) | copy-start | bytes 25165828
  211.7 4.8 %copy-start.5 = (bf16[512,16,128]{0,2,1:T(8,128)(2,1)S(1)}, bf16[512,16,128]{0,2,1:T(8,128)(2,1)}, u32[]{:S(2)}) copy-start(bf16[512,16,128]{0,2,1:T(8,128)(2,1)} %copy.103) | copy-start | bytes 6291460
  286.9 3.4 %copy-start.4 = (f32[16,128,512]{2,1,0:T(8,128)S(1)}, f32[16,128,512]{2,1,0:T(8,128)}, u32[]{:S(2)}) copy-start(f32[16,128,512]{2,1,0:T(8,128)} %fusion.50) | copy-start | bytes 12582916
  286.9 4.4 %copy-start.10 = (bf16[512,2048]{1,0:T(8,128)(2,1)S(1)}, bf16[512,2048]{1,0:T(8,128)(2,1)}, u32[]{:S(2)}) copy-start(bf16[512,2048]{1,0:T(8,128)(2,1)} %param.9) | copy-start | bytes 6291460
Sparse Core Ops, SparseCore 0:
  18.4 75.5 all-gather.4
  203.3 70.4 all-gather.6
where the time goes:
time: 318 us; the launch traced here: 316 us
  waiting for transfers between devices  122 us (38%)
  local copies, waits for them, and re-layouts  60.3 us (19%)
  matrix products  51.3 us (16%)
  other arithmetic  33.6 us (11%)
  blocking collectives  29.2 us (9%)
  between operations  14.2 us (4%)
  starting transfers between devices  4.72 us (1%)
    all_gather x1, waiting for transfers between devices, on_device(): lax.all_gather(local_state[None].astype(jnp.bfloat16), 'seq', axis=0, til...  63.4 us
    all_gather x1, waiting for transfers between devices, carried_in(): everything = lax.all_gather(value.astype(jnp.bfloat16), axis)  41.6 us
    unnamed x34, local copies, waits for them, and re-layouts  34.6 us
    all_to_all x1, blocking collectives, on_device(): lax.all_to_all(grad_rows, 'head', split_axis=1, concat_axis=0, tiled=True)  29.2 us
    all_to_all x1, waiting for transfers between devices, on_device(): lax.all_to_all(attn_out, 'head', split_axis=0, concat_axis=1, tiled=True)  17.4 us
    select_n x8, other arithmetic, step(): return jnp.where(reached, new, before)  12.9 us
    reshape x2, local copies, waits for them, and re-layouts, split_heads(): matrix.reshape(matrix.shape[0], matrix.shape[1] // head_dim, head_dim)  8.6 us
    dot_general x1, matrix products, on_device(): jnp.einsum('hts,thd->shd', grad_scores, queries, preferred_element_type=j...  7.93 us
  transfers between devices with their start and end apart: 3, of which 3 were waited for; matrix products, arithmetic and copies ran while one was open for 15% of the time, Pallas kernels for 0%

commit v1 on v0

v1 whole, which is shorter than its diff:
```python
import functools

import jax
import jax.numpy as jnp
from jax import lax
from jax.experimental import pallas as pl
from jax.experimental.pallas import tpu as pltpu
from jax.sharding import PartitionSpec as P

HEAD_DIM = 128
EPS = 1e-06
MESH = pl.DeviceIdType.MESH
F32 = jnp.float32
BF16 = jnp.bfloat16


def dot_nn(a, b):
    return lax.dot_general(a, b, (((1,), (0,)), ((), ())), preferred_element_type=F32)


def dot_nt(a, b):
    return lax.dot_general(a, b, (((1,), (1,)), ((), ())), preferred_element_type=F32)


def dot_tn(a, b):
    return lax.dot_general(a, b, (((0,), (0,)), ((), ())), preferred_element_type=F32)


def body(
    n_seq, n_head,
    q_h, k_h, v_h, gate_h, gain_h, go_h,
    gq_h, gk_h, gv_h, gg_h,
    q, k, v, gate, gain, go,
    wsend, wbuf, g2, attn, d_o, arows,
    st, st_p, st_c, st_o, pre,
    gst, gst_p, gst_c, gst_o,
    zbuf, stat_s, stat_r, inv_b, c_b,
    gqv, gkv, gvv, ggv,
    in_sem, out_sem, gg_sem,
    w_ss, w_rs, a_ss, a_rs, s_ss, s_rs,
    p_ss, p_rs, c_ss, c_rs, gp_ss, gp_rs, gc_ss, gc_rs,
):
    hd = HEAD_DIM
    tok, cols = q.shape
    rows, width = gate.shape
    heads = cols // hd
    half = tok // 2
    idx = lax.axis_index("seq")
    me = lax.axis_index("head")
    side = lax.rem(idx, 2)
    partner = idx + 1 - 2 * side
    has_below = idx >= 2
    has_above = idx + 2 < n_seq
    order = [n_head // 2] + [d for d in range(1, n_head) if d != n_head // 2]

    def to_peer(d):
        return lax.rem(me + d, n_head)

    def from_peer(d):
        return lax.rem(me + n_head - d, n_head)

    loads = [
        pltpu.make_async_copy(src, dst, in_sem.at[i])
        for i, (src, dst) in enumerate(
            ((gain_h, gain), (gate_h, gate), (go_h, go), (k_h, k), (v_h, v), (q_h, q))
        )
    ]
    for load in loads:
        load.start()

    barrier = pltpu.get_barrier_semaphore()
    for d in range(1, n_head):
        pl.semaphore_signal(barrier, inc=1, device_id={"head": to_peer(d)}, device_id_type=MESH)
    pl.semaphore_signal(barrier, inc=1, device_id={"seq": partner}, device_id_type=MESH)

    @pl.when(has_below)
    def _():
        pl.semaphore_signal(barrier, inc=1, device_id={"seq": idx - 2}, device_id_type=MESH)

    @pl.when(has_above)
    def _():
        pl.semaphore_signal(barrier, inc=1, device_id={"seq": idx + 2}, device_id_type=MESH)

    below, above = has_below.astype(jnp.int32), has_above.astype(jnp.int32)
    pl.semaphore_wait(barrier, n_head + below + above)

    def head_cols(h):
        return pl.ds(pl.multiple_of(h * hd, hd), hd)

    br, bc = 32, 512
    n_bc = cols // bc
    n_blocks = (rows // br) * n_bc

    def block_at(i, start):
        r = pl.multiple_of((i // n_bc) * br, br)
        c = lax.rem(i, n_bc) * bc
        return r, pl.multiple_of(c, bc), pl.multiple_of(start + c, bc)

    def weigh(shard, local):
        start = shard * cols

        def step(i, carry):
            r, c, at = block_at(i, start)
            g = gate[pl.ds(r, br), pl.ds(at, bc)].astype(F32)
            scaled = go[pl.ds(r, br), pl.ds(at, bc)].astype(F32) * gain[:, pl.ds(at, bc)]
            sig = jax.nn.sigmoid(g)
            part = scaled * sig
            g2[pl.ds(r, br), pl.ds(at, bc)] = part * (1.0 + g * (1.0 - sig))
            weighted = (part * g).astype(BF16)
            if local:
                wbuf[pl.ds(pl.multiple_of(me * rows + r, br), br), pl.ds(c, bc)] = weighted
            else:
                wsend[pl.ds(r, br), pl.ds(at, bc)] = weighted
            return carry

        lax.fori_loop(0, n_blocks, step, 0)

    def row_block(shard):
        return pl.ds(pl.multiple_of(shard * rows, rows), rows)

    def col_block(shard):
        return pl.ds(pl.multiple_of(shard * cols, cols), cols)

    def w_copy(d):
        return pltpu.make_async_remote_copy(
            src_ref=wsend.at[:, col_block(to_peer(d))],
            dst_ref=wbuf.at[row_block(me), :],
            send_sem=w_ss.at[d], recv_sem=w_rs.at[d],
            device_id={"head": to_peer(d)}, device_id_type=MESH,
        )

    def w_arrival(d):
        return pltpu.make_async_remote_copy(
            src_ref=wsend.at[:, col_block(to_peer(d))],
            dst_ref=wbuf.at[row_block(from_peer(d)), :],
            send_sem=w_ss.at[d], recv_sem=w_rs.at[d],
            device_id={"head": to_peer(d)}, device_id_type=MESH,
        )

    def a_copy(d):
        return pltpu.make_async_remote_copy(
            src_ref=attn.at[row_block(to_peer(d)), :],
            dst_ref=arows.at[:, col_block(me)],
            send_sem=a_ss.at[d], recv_sem=a_rs.at[d],
            device_id={"head": to_peer(d)}, device_id_type=MESH,
        )

    def a_arrival(d):
        return pltpu.make_async_remote_copy(
            src_ref=attn.at[row_block(to_peer(d)), :],
            dst_ref=arows.at[:, col_block(from_peer(d))],
            send_sem=a_ss.at[d], recv_sem=a_rs.at[d],
            device_id={"head": to_peer(d)}, device_id_type=MESH,
        )

    def s_copy(d):
        return pltpu.make_async_remote_copy(
            src_ref=stat_s, dst_ref=stat_r.at[d],
            send_sem=s_ss.at[d], recv_sem=s_rs.at[d],
            device_id={"head": to_peer(d)}, device_id_type=MESH,
        )

    def state_copy(src, dst, ss, rs, h, target):
        return pltpu.make_async_remote_copy(
            src_ref=src.at[h], dst_ref=dst.at[h],
            send_sem=ss.at[h], recv_sem=rs.at[h],
            device_id={"seq": target}, device_id_type=MESH,
        )

    for load in loads[:3]:
        load.wait()
    for d in order[:1]:
        weigh(to_peer(d), False)
        w_copy(d).start()

    for load in loads[3:5]:
        load.wait()

    def send_state(h, carry):
        sl = head_cols(h)
        st[h] = dot_tn(k[:, sl], v[:, sl]).astype(BF16)
        state_copy(st, st_p, p_ss, p_rs, h, partner).start()
        return carry

    lax.fori_loop(0, heads, send_state, 0)

    for d in order[1:]:
        weigh(to_peer(d), False)
        w_copy(d).start()
    weigh(me, True)
    loads[5].wait()

    def pass_on(h, own, mate, chain, out, sems, source_ok, target_ok, target, wants_mate):
        mate_ss, mate_rs, chain_ss, chain_rs = sems
        state_copy(own, mate, mate_ss, mate_rs, h, partner).wait_recv()
        got = mate[h].astype(F32)

        @pl.when(source_ok)
        def _():
            state_copy(out, chain, chain_ss, chain_rs, h, target).wait_recv()

        @pl.when(jnp.logical_not(source_ok))
        def _():
            chain[h] = jnp.zeros((hd, hd), BF16)

        before = chain[h].astype(F32)

        @pl.when(target_ok)
        def _():
            out[h] = (before + got + own[h].astype(F32)).astype(BF16)
            state_copy(out, chain, chain_ss, chain_rs, h, target).start()

        return (before + wants_mate.astype(F32) * got).astype(BF16)

    at_row = lax.broadcasted_iota(jnp.int32, (half, half), 0)
    at_col = lax.broadcasted_iota(jnp.int32, (half, half), 1)

    def lower(x):
        return jnp.where(at_row >= at_col, x, 0.0).astype(BF16)

    def upper(x):
        return jnp.where(at_row <= at_col, x, 0.0).astype(BF16)

    def forward(h, carry):
        sl = head_cols(h)
        q0, q1 = q[:half, sl], q[half:, sl]
        k0, k1 = k[:half, sl], k[half:, sl]
        v0, v1 = v[:half, sl], v[half:, sl]
        o0 = dot_nn(lower(dot_nt(q0, k0)), v0)
        o1 = dot_nn(dot_nt(q1, k0).astype(BF16), v0) + dot_nn(lower(dot_nt(q1, k1)), v1)
        before = pass_on(
            h, st, st_p, st_c, st_o, (p_ss, p_rs, c_ss, c_rs),
            has_below, has_above, idx + 2, side,
        )
        pre[h] = before
        attn[:half, sl] = (o0 + dot_nn(q0, before)).astype(BF16)
        attn[half:, sl] = (o1 + dot_nn(q1, before)).astype(BF16)
        return carry

    lax.fori_loop(0, heads, forward, 0)

    for d in order:
        w_arrival(d).wait_recv()

    lane = lax.broadcasted_iota(jnp.int32, (64, hd), 1)

    def sums(i, carry):
        rs = pl.ds(pl.multiple_of(i * 64, 64), 64)
        squares = jnp.zeros((64, hd), F32)
        crossed = jnp.zeros((64, hd), F32)
        for h in range(heads):
            a = attn[rs, h * hd:(h + 1) * hd].astype(F32)
            w = wbuf[rs, h * hd:(h + 1) * hd].astype(F32)
            squares = squares + a * a
            crossed = crossed + a * w
        s0 = jnp.sum(squares, axis=1, keepdims=True)
        s1 = jnp.sum(crossed, axis=1, keepdims=True)
        zbuf[rs, :] = jnp.where(lane == 0, s0, jnp.where(lane == 1, s1, 0.0))
        return carry

    lax.fori_loop(0, tok // 64, sums, 0)
    stat_s[...] = jnp.transpose(zbuf[...])[:8]
    for d in order:
        s_copy(d).start()
    for d in order:
        a_copy(d).start()
    total = stat_s[...]
    for d in order:
        s_copy(d).wait_recv()
        total = total + stat_r[d]
    spread = jnp.transpose(jnp.concatenate([total, jnp.zeros((hd - 8, tok), F32)], axis=0))
    inv = lax.rsqrt(spread[:, 0:1] / width + EPS)
    inv_b[...] = jnp.broadcast_to(inv, (tok, hd))
    c_b[...] = jnp.broadcast_to(inv * inv * (spread[:, 1:2] / width), (tok, hd))

    def send_grad(h, carry):
        sl = head_cols(h)
        a = attn[:, sl].astype(F32)
        grad = (inv_b[...] * (wbuf[:, sl].astype(F32) - a * c_b[...])).astype(BF16)
        d_o[:, sl] = grad
        gst[h] = dot_tn(q[:, sl], grad).astype(BF16)
        state_copy(gst, gst_p, gp_ss, gp_rs, h, partner).start()
        return carry

    lax.fori_loop(0, heads, send_grad, 0)

    def out_copies(h):
        sl = head_cols(h)
        return [
            pltpu.make_async_copy(src.at[:, sl], dst.at[:, sl], out_sem.at[i, h])
            for i, (src, dst) in enumerate(((gqv, gq_h), (gkv, gk_h), (gvv, gv_h)))
        ]

    def backward(h, carry):
        sl = head_cols(h)
        q0, q1 = q[:half, sl], q[half:, sl]
        k0, k1 = k[:half, sl], k[half:, sl]
        v0, v1 = v[:half, sl], v[half:, sl]
        d0, d1 = d_o[:half, sl], d_o[half:, sl]
        before = pre[h]
        gqv[:half, sl] = (dot_nn(lower(dot_nt(d0, v0)), k0) + dot_nt(d0, before)).astype(BF16)
        gqv[half:, sl] = (
            dot_nn(dot_nt(d1, v0).astype(BF16), k0)
            + dot_nn(lower(dot_nt(d1, v1)), k1)
            + dot_nt(d1, before)
        ).astype(BF16)
        gk0 = dot_nn(upper(dot_nt(v0, d0)), q0) + dot_nn(dot_nt(v0, d1).astype(BF16), q1)
        gk1 = dot_nn(upper(dot_nt(v1, d1)), q1)
        gv0 = dot_nn(upper(dot_nt(k0, q0)), d0) + dot_nn(dot_nt(k0, q1).astype(BF16), d1)
        gv1 = dot_nn(upper(dot_nt(k1, q1)), d1)
        after = pass_on(
            h, gst, gst_p, gst_c, gst_o, (gp_ss, gp_rs, gc_ss, gc_rs),
            has_above, has_below, idx - 2, 1 - side,
        )
        gkv[:half, sl] = (gk0 + dot_nt(v0, after)).astype(BF16)
        gkv[half:, sl] = (gk1 + dot_nt(v1, after)).astype(BF16)
        gvv[:half, sl] = (gv0 + dot_nn(k0, after)).astype(BF16)
        gvv[half:, sl] = (gv1 + dot_nn(k1, after)).astype(BF16)
        for copy in out_copies(h):
            copy.start()
        return carry

    lax.fori_loop(0, heads, backward, 0)

    def gg_copy(shard, d):
        return pltpu.make_async_copy(
            ggv.at[:, col_block(shard)], gg_h.at[:, col_block(shard)], gg_sem.at[d]
        )

    def finish(shard, local):
        start = shard * cols

        def step(i, carry):
            r, c, at = block_at(i, start)
            mine = pl.multiple_of(me * rows + r, br)
            if local:
                a = attn[pl.ds(mine, br), pl.ds(c, bc)]
            else:
                a = arows[pl.ds(r, br), pl.ds(at, bc)]
            scale = inv_b[pl.ds(mine, br), :][:, 0:1]
            ggv[pl.ds(r, br), pl.ds(at, bc)] = (
                g2[pl.ds(r, br), pl.ds(at, bc)] * (a.astype(F32) * scale)
            ).astype(BF16)
            return carry

        lax.fori_loop(0, n_blocks, step, 0)

    finish(me, True)
    gg_copy(me, 0).start()
    for d in order:
        a_arrival(d).wait_recv()
        finish(from_peer(d), False)
        gg_copy(from_peer(d), d).start()

    gg_copy(me, 0).wait()
    for d in order:
        gg_copy(from_peer(d), d).wait()
        w_copy(d).wait_send()
        s_copy(d).wait_send()
        a_copy(d).wait_send()

    def drain(h, carry):
        for copy in out_copies(h):
            copy.wait()
        state_copy(st, st_p, p_ss, p_rs, h, partner).wait_send()
        state_copy(gst, gst_p, gp_ss, gp_rs, h, partner).wait_send()

        @pl.when(has_above)
        def _():
            state_copy(st_o, st_c, c_ss, c_rs, h, idx + 2).wait_send()

        @pl.when(has_below)
        def _():
            state_copy(gst_o, gst_c, gc_ss, gc_rs, h, idx - 2).wait_send()

        return carry

    lax.fori_loop(0, heads, drain, 0)


def on_device(n_seq, n_head, query, key_in, value, gate, gain, grad_out):
    tok, cols = query.shape
    rows, width = gate.shape
    heads = cols // HEAD_DIM
    wide = pltpu.VMEM((tok, cols), BF16)
    thin = pltpu.VMEM((rows, width), BF16)
    state = pltpu.VMEM((heads, HEAD_DIM, HEAD_DIM), BF16)
    token = pltpu.VMEM((tok, HEAD_DIM), F32)
    by_peer = pltpu.SemaphoreType.DMA((n_head,))
    by_head = pltpu.SemaphoreType.DMA((heads,))
    anywhere = pl.BlockSpec(memory_space=pl.ANY)
    return pl.pallas_call(
        functools.partial(body, n_seq, n_head),
        out_shape=[jax.ShapeDtypeStruct((tok, cols), BF16)] * 3
        + [jax.ShapeDtypeStruct((rows, width), BF16)],
        in_specs=[anywhere] * 6,
        out_specs=[anywhere] * 4,
        scratch_shapes=[
            wide, wide, wide, thin, pltpu.VMEM((1, width), F32), thin,
            thin, wide, pltpu.VMEM((rows, width), F32), wide, wide, thin,
            state, state, state, state, state,
            state, state, state, state,
            token, pltpu.VMEM((8, tok), F32), pltpu.VMEM((n_head, 8, tok), F32), token, token,
            wide, wide, wide, thin,
            pltpu.SemaphoreType.DMA((6,)), pltpu.SemaphoreType.DMA((3, heads)), by_peer,
            by_peer, by_peer, by_peer, by_peer, by_peer, by_peer,
            by_head, by_head, by_head, by_head, by_head, by_head, by_head, by_head,
        ],
        compiler_params=pltpu.CompilerParams(
            collective_id=0, has_side_effects=True, vmem_limit_bytes=60 * 2**20
        ),
        name="linear_attention_backward",
    )(query, key_in, value, gate, gain.reshape(1, width), grad_out)


def solution(mesh):
    in_specs = (
        P("seq", "head"),
        P("seq", "head"),
        P("seq", "head"),
        P(("seq", "head"), None),
        P(),
        P(("seq", "head"), None),
    )
    out_specs = (P("seq", "head"), P("seq", "head"), P("seq", "head"), P(("seq", "head"), None))
    return jax.shard_map(
        functools.partial(on_device, mesh.shape["seq"], mesh.shape["head"]),
        mesh=mesh, in_specs=in_specs, out_specs=out_specs, check_vma=False,
    )
```

time: 318 us -> 91.7 us (0.29)
  waiting for transfers between devices: 122 us -> 0 us
  Pallas kernels: 0 us -> 81.5 us
  matrix products: 51.3 us -> 0 us
  local copies, waits for them, and re-layouts: 60.3 us -> 9.32 us
  other arithmetic: 33.6 us -> 0 us
  blocking collectives: 29.2 us -> 0 us
  between operations: 14.2 us -> 0.65 us
  starting transfers between devices: 4.72 us -> 0 us
    all_gather x2 -> x0, waiting for transfers between devices: 105 us -> none  [the longest x1 63.4 us: on_device(): lax.all_gather(local_state[None].astype(jnp.bfloat16), 'seq', axis=0, til...]
    pallas_call x0 -> x1, Pallas kernels: none -> 81.5 us  [on_device(): pl.pallas_call(functools.partial(body, n_seq, n_head), out_shape=[jax.Sha...]
    dot_general x12 -> x0, matrix products: 51.3 us -> none  [the longest x1 7.93 us: on_device(): jnp.einsum('hts,thd->shd', grad_scores, queries, preferred_element_type=j...]
    all_to_all x1 -> x0, blocking collectives: 29.2 us -> none  [on_device(): lax.all_to_all(grad_rows, 'head', split_axis=1, concat_axis=0, tiled=True)]
    unnamed x34 -> x10, local copies, waits for them, and re-layouts: 34.6 us -> 9.32 us
    all_to_all x1 -> x0, waiting for transfers between devices: 17.4 us -> none  [on_device(): lax.all_to_all(attn_out, 'head', split_axis=0, concat_axis=1, tiled=True)]
    select_n x8 -> x0, other arithmetic: 12.9 us -> none  [step(): return jnp.where(reached, new, before)]
    reduce_sum x3 -> x0, other arithmetic: 12.1 us -> none  [the longest x1 6.72 us: on_device(): jnp.mean(weighted * normed, axis=1, keepdims=True)]
  transfers between devices with their start and end apart: 3 -> 0, of which waited for: 3 -> 0; matrix products, arithmetic and copies ran while one was open for 15% -> 0% of each run, Pallas kernels for 0% -> 0%
where the time goes in v1:
time: 91.7 us; the launch traced here: 91.5 us
  Pallas kernels  81.5 us (89%)
  local copies, waits for them, and re-layouts  9.32 us (10%)
    pallas_call x1, Pallas kernels, on_device(): pl.pallas_call(functools.partial(body, n_seq, n_head), out_shape=[jax.Sha...  81.5 us
    unnamed x10, local copies, waits for them, and re-layouts  9.32 us

profile of v1, /device:TPU:0, one launch (start us, length us, event | category | flops | bytes accessed | tf_op | source)
XLA Modules:
  0.0 91.5 jit_solution(15208881619439514740)
XLA Ops:
  0.6 81.5 %linear_attention_backward.1 = (bf16[512,2048]{1,0:T(8,128)(2,1)}, bf16[512,2048]{1,0:T(8,128)(2,1)}, bf16[512,2048]{1,0:T(8,128)(2,1)}, bf16[128,8192]{1,0:T(8,128)(2,1)}) custom-call(bf16[512,2048]{1,0:T(8,128)(2,1)} %q_h.1, bf16[512,2048]{1,0:T(8,128)(2,1)} %k_h.1, bf16[512,2048]{1,0:T(8,128)(2,1)} %v_h.1, bf16[128,8192]{1,0:T(8,128)(2,1)} %gate_h.1, ...), custom_call_target="tpu_custom_call" | custom-call | tf_op jit(solution)/shard_map/linear_attention_backward/pallas_call | solution.py:392
  82.1 0.0 copy-start.2
  82.1 3.3 %copy.14 = bf16[512,2048]{1,0:T(8,128)(2,1)} copy(bf16[512,2048]{1,0:T(8,128)(2,1)} %get-tuple-element.8) | data formatting | bytes 4194304
  85.5 0.0 copy-done.2
  85.5 0.0 copy-start.1
  85.5 1.3 %copy.15 = bf16[512,2048]{1,0:T(8,128)(2,1)} copy(bf16[512,2048]{1,0:T(8,128)(2,1)S(1)} %copy-done.2) | data formatting | bytes 4194304
  86.8 1.0 %copy-done.1 = bf16[512,2048]{1,0:T(8,128)(2,1)S(1)} copy-done((bf16[512,2048]{1,0:T(8,128)(2,1)S(1)}, bf16[512,2048]{1,0:T(8,128)(2,1)}, u32[]{:S(2)}) %copy-start.1) | copy-done | bytes 2097176
  87.8 0.0 copy-start
  87.8 1.3 %copy.16 = bf16[512,2048]{1,0:T(8,128)(2,1)} copy(bf16[512,2048]{1,0:T(8,128)(2,1)S(1)} %copy-done.1) | data formatting | bytes 4194304
  89.1 1.0 %copy-done = bf16[128,8192]{1,0:T(8,128)(2,1)S(1)} copy-done((bf16[128,8192]{1,0:T(8,128)(2,1)S(1)}, bf16[128,8192]{1,0:T(8,128)(2,1)}, u32[]{:S(2)}) %copy-start) | copy-done | bytes 2097176
  90.2 1.3 %copy.17 = bf16[128,8192]{1,0:T(8,128)(2,1)} copy(bf16[128,8192]{1,0:T(8,128)(2,1)S(1)} %copy-done) | data formatting | bytes 4194304
Async XLA Ops:
  82.1 3.3 %copy-start.2 = (bf16[512,2048]{1,0:T(8,128)(2,1)S(1)}, bf16[512,2048]{1,0:T(8,128)(2,1)}, u32[]{:S(2)}) copy-start(bf16[512,2048]{1,0:T(8,128)(2,1)} %get-tuple-element.9) | copy-start | bytes 6291460
  85.5 2.3 %copy-start.1 = (bf16[512,2048]{1,0:T(8,128)(2,1)S(1)}, bf16[512,2048]{1,0:T(8,128)(2,1)}, u32[]{:S(2)}) copy-start(bf16[512,2048]{1,0:T(8,128)(2,1)} %get-tuple-element.10) | copy-start | bytes 6291460
  87.8 2.3 %copy-start = (bf16[128,8192]{1,0:T(8,128)(2,1)S(1)}, bf16[128,8192]{1,0:T(8,128)(2,1)}, u32[]{:S(2)}) copy-start(bf16[128,8192]{1,0:T(8,128)(2,1)} %get-tuple-element.11) | copy-start | bytes 6291460

commit v2 on v1

--- a/solution.py
+++ b/solution.py
@@ -12,6 +12,8 @@
 MESH = pl.DeviceIdType.MESH
 F32 = jnp.float32
 BF16 = jnp.bfloat16
+FORWARD_LAG = 4
+BACKWARD_LAG = 2
 
 
 def dot_nn(a, b):
@@ -29,14 +31,14 @@
 def body(
     n_seq, n_head,
     q_h, k_h, v_h, gate_h, gain_h, go_h,
-    gq_h, gk_h, gv_h, gg_h,
+    gqv, gkv, gvv, ggv,
     q, k, v, gate, gain, go,
     wsend, wbuf, g2, attn, d_o, arows,
     st, st_p, st_c, st_o, pre,
     gst, gst_p, gst_c, gst_o,
+    suf, scores, acc_a, acc_b,
     zbuf, stat_s, stat_r, inv_b, c_b,
-    gqv, gkv, gvv, ggv,
-    in_sem, out_sem, gg_sem,
+    in_sem,
     w_ss, w_rs, a_ss, a_rs, s_ss, s_rs,
     p_ss, p_rs, c_ss, c_rs, gp_ss, gp_rs, gc_ss, gc_rs,
 ):
@@ -221,23 +223,42 @@
     def upper(x):
         return jnp.where(at_row <= at_col, x, 0.0).astype(BF16)
 
-    def forward(h, carry):
+    depth = idx // 2
+    pairs = n_seq // 2
+
+    def forward_local(h):
         sl = head_cols(h)
         q0, q1 = q[:half, sl], q[half:, sl]
         k0, k1 = k[:half, sl], k[half:, sl]
         v0, v1 = v[:half, sl], v[half:, sl]
-        o0 = dot_nn(lower(dot_nt(q0, k0)), v0)
-        o1 = dot_nn(dot_nt(q1, k0).astype(BF16), v0) + dot_nn(lower(dot_nt(q1, k1)), v1)
-        before = pass_on(
-            h, st, st_p, st_c, st_o, (p_ss, p_rs, c_ss, c_rs),
-            has_below, has_above, idx + 2, side,
-        )
-        pre[h] = before
-        attn[:half, sl] = (o0 + dot_nn(q0, before)).astype(BF16)
-        attn[half:, sl] = (o1 + dot_nn(q1, before)).astype(BF16)
-        return carry
-
-    lax.fori_loop(0, heads, forward, 0)
+        acc_a[:half, sl] = dot_nn(lower(dot_nt(q0, k0)), v0)
+        acc_a[half:, sl] = dot_nn(dot_nt(q1, k0).astype(BF16), v0) + dot_nn(
+            lower(dot_nt(q1, k1)), v1
+        )
+        scores[h, 0] = upper(dot_nt(k0, q0))
+        scores[h, 1] = dot_nt(k0, q1).astype(BF16)
+        scores[h, 2] = upper(dot_nt(k1, q1))
+
+    def forward(i, carry):
+        @pl.when(i < heads)
+        def _():
+            forward_local(i)
+
+        h = i - FORWARD_LAG * depth
+
+        @pl.when((h >= 0) & (h < heads))
+        def _():
+            sl = head_cols(h)
+            before = pass_on(
+                h, st, st_p, st_c, st_o, (p_ss, p_rs, c_ss, c_rs),
+                has_below, has_above, idx + 2, side,
+            )
+            pre[h] = before
+            attn[:, sl] = (acc_a[:, sl] + dot_nn(q[:, sl], before)).astype(BF16)
+
+        return carry
+
+    lax.fori_loop(0, heads + FORWARD_LAG * (pairs - 1), forward, 0)
 
     for d in order:
         w_arrival(d).wait_recv()
@@ -284,14 +305,7 @@
 
     lax.fori_loop(0, heads, send_grad, 0)
 
-    def out_copies(h):
-        sl = head_cols(h)
-        return [
-            pltpu.make_async_copy(src.at[:, sl], dst.at[:, sl], out_sem.at[i, h])
-            for i, (src, dst) in enumerate(((gqv, gq_h), (gkv, gk_h), (gvv, gv_h)))
-        ]
-
-    def backward(h, carry):
+    def backward_local(h):
         sl = head_cols(h)
         q0, q1 = q[:half, sl], q[half:, sl]
         k0, k1 = k[:half, sl], k[half:, sl]
@@ -304,28 +318,41 @@
             + dot_nn(lower(dot_nt(d1, v1)), k1)
             + dot_nt(d1, before)
         ).astype(BF16)
-        gk0 = dot_nn(upper(dot_nt(v0, d0)), q0) + dot_nn(dot_nt(v0, d1).astype(BF16), q1)
-        gk1 = dot_nn(upper(dot_nt(v1, d1)), q1)
-        gv0 = dot_nn(upper(dot_nt(k0, q0)), d0) + dot_nn(dot_nt(k0, q1).astype(BF16), d1)
-        gv1 = dot_nn(upper(dot_nt(k1, q1)), d1)
-        after = pass_on(
-            h, gst, gst_p, gst_c, gst_o, (gp_ss, gp_rs, gc_ss, gc_rs),
-            has_above, has_below, idx - 2, 1 - side,
-        )
-        gkv[:half, sl] = (gk0 + dot_nt(v0, after)).astype(BF16)
-        gkv[half:, sl] = (gk1 + dot_nt(v1, after)).astype(BF16)
-        gvv[:half, sl] = (gv0 + dot_nn(k0, after)).astype(BF16)
-        gvv[half:, sl] = (gv1 + dot_nn(k1, after)).astype(BF16)
-        for copy in out_copies(h):
-            copy.start()
-        return carry
-
-    lax.fori_loop(0, heads, backward, 0)
-
-    def gg_copy(shard, d):
-        return pltpu.make_async_copy(
-            ggv.at[:, col_block(shard)], gg_h.at[:, col_block(shard)], gg_sem.at[d]
-        )
+        acc_a[:half, sl] = dot_nn(upper(dot_nt(v0, d0)), q0) + dot_nn(
+            dot_nt(v0, d1).astype(BF16), q1
+        )
+        acc_a[half:, sl] = dot_nn(upper(dot_nt(v1, d1)), q1)
+        acc_b[:half, sl] = dot_nn(scores[h, 0], d0) + dot_nn(scores[h, 1], d1)
+        acc_b[half:, sl] = dot_nn(scores[h, 2], d1)
+
+    def backward(i, carry):
+        @pl.when(i < heads)
+        def _():
+            backward_local(i)
+
+        for t in range(2):
+            h = 2 * (i - BACKWARD_LAG * (pairs - 1 - depth)) + t
+
+            @pl.when((h >= 0) & (h < heads))
+            def _():
+                suf[h] = pass_on(
+                    h, gst, gst_p, gst_c, gst_o, (gp_ss, gp_rs, gc_ss, gc_rs),
+                    has_above, has_below, idx - 2, 1 - side,
+                )
+
+        return carry
+
+    steps = max(heads, BACKWARD_LAG * (pairs - 1) + (heads + 1) // 2)
+    lax.fori_loop(0, steps, backward, 0)
+
+    def add_later(h, carry):
+        sl = head_cols(h)
+        after = suf[h]
+        gkv[:, sl] = (acc_a[:, sl] + dot_nt(v[:, sl], after)).astype(BF16)
+        gvv[:, sl] = (acc_b[:, sl] + dot_nn(k[:, sl], after)).astype(BF16)
+        return carry
+
+    lax.fori_loop(0, heads, add_later, 0)
 
     def finish(shard, local):
         start = shard * cols
@@ -346,22 +373,16 @@
         lax.fori_loop(0, n_blocks, step, 0)
 
     finish(me, True)
-    gg_copy(me, 0).start()
     for d in order:
         a_arrival(d).wait_recv()
         finish(from_peer(d), False)
-        gg_copy(from_peer(d), d).start()
-
-    gg_copy(me, 0).wait()
-    for d in order:
-        gg_copy(from_peer(d), d).wait()
+
+    for d in order:
         w_copy(d).wait_send()
         s_copy(d).wait_send()
         a_copy(d).wait_send()
 
     def drain(h, carry):
-        for copy in out_copies(h):
-            copy.wait()
         state_copy(st, st_p, p_ss, p_rs, h, partner).wait_send()
         state_copy(gst, gst_p, gp_ss, gp_rs, h, partner).wait_send()
 
@@ -376,6 +397,17 @@
         return carry
 
     lax.fori_loop(0, heads, drain, 0)
+
+
+def store(a, b, c, d, a_h, b_h, c_h, d_h, sem):
+    copies = [
+        pltpu.make_async_copy(src, dst, sem.at[i])
+        for i, (src, dst) in enumerate(((a, a_h), (b, b_h), (c, c_h), (d, d_h)))
+    ]
+    for copy in copies:
+        copy.start()
+    for copy in copies:
+        copy.wait()
 
 
 def on_device(n_seq, n_head, query, key_in, value, gate, gain, grad_out):
@@ -389,28 +421,38 @@
     by_peer = pltpu.SemaphoreType.DMA((n_head,))
     by_head = pltpu.SemaphoreType.DMA((heads,))
     anywhere = pl.BlockSpec(memory_space=pl.ANY)
-    return pl.pallas_call(
+    on_chip = pl.BlockSpec(memory_space=pltpu.VMEM)
+    sum_of = pltpu.VMEM((tok, cols), F32)
+    results = pl.pallas_call(
         functools.partial(body, n_seq, n_head),
-        out_shape=[jax.ShapeDtypeStruct((tok, cols), BF16)] * 3
-        + [jax.ShapeDtypeStruct((rows, width), BF16)],
+        out_shape=[wide, wide, wide, thin],
         in_specs=[anywhere] * 6,
-        out_specs=[anywhere] * 4,
+        out_specs=[on_chip] * 4,
         scratch_shapes=[
             wide, wide, wide, thin, pltpu.VMEM((1, width), F32), thin,
             thin, wide, pltpu.VMEM((rows, width), F32), wide, wide, thin,
             state, state, state, state, state,
             state, state, state, state,
+            state, pltpu.VMEM((heads, 3, tok // 2, tok // 2), BF16), sum_of, sum_of,
             token, pltpu.VMEM((8, tok), F32), pltpu.VMEM((n_head, 8, tok), F32), token, token,
-            wide, wide, wide, thin,
-            pltpu.SemaphoreType.DMA((6,)), pltpu.SemaphoreType.DMA((3, heads)), by_peer,
+            pltpu.SemaphoreType.DMA((6,)),
             by_peer, by_peer, by_peer, by_peer, by_peer, by_peer,
             by_head, by_head, by_head, by_head, by_head, by_head, by_head, by_head,
         ],
         compiler_params=pltpu.CompilerParams(
-            collective_id=0, has_side_effects=True, vmem_limit_bytes=60 * 2**20
+            collective_id=0, has_side_effects=True, vmem_limit_bytes=52 * 2**20
         ),
         name="linear_attention_backward",
     )(query, key_in, value, gate, gain.reshape(1, width), grad_out)
+    return pl.pallas_call(
+        store,
+        out_shape=[jax.ShapeDtypeStruct(x.shape, BF16) for x in results],
+        in_specs=[on_chip] * 4,
+        out_specs=[anywhere] * 4,
+        scratch_shapes=[pltpu.SemaphoreType.DMA((4,))],
+        compiler_params=pltpu.CompilerParams(vmem_limit_bytes=2**20),
+        name="store_gradients",
+    )(*[pltpu.with_memory_space_constraint(x, pltpu.VMEM) for x in results])
 
 
 def solution(mesh):

time: 91.7 us -> 80.6 us (0.88)
  local copies, waits for them, and re-layouts: 9.32 us -> 0 us
  Pallas kernels: 81.5 us -> 79.8 us
    unnamed x10 -> x0, local copies, waits for them, and re-layouts: 9.32 us -> none
    pallas_call x1 -> x2, Pallas kernels: 81.5 us -> 79.8 us  [the longest x1 76.4 us: on_device(): pl.pallas_call(functools.partial(body, n_seq, n_head), out_shape=[wide, w...]
where the time goes in v2:
time: 80.6 us; the launch traced here: 80.4 us
  Pallas kernels  79.8 us (99%)
    pallas_call x1, Pallas kernels, on_device(): pl.pallas_call(functools.partial(body, n_seq, n_head), out_shape=[wide, w...  76.4 us
    pallas_call x1, Pallas kernels, on_device(): pl.pallas_call(store, out_shape=[jax.ShapeDtypeStruct(x.shape, BF16) for...  3.37 us

profile of v2, /device:TPU:0, one launch (start us, length us, event | category | flops | bytes accessed | tf_op | source)
XLA Modules:
  0.0 80.4 jit_solution(15189633603538398222)
XLA Ops:
  0.6 76.4 %linear_attention_backward.1 = (bf16[512,2048]{1,0:T(8,128)(2,1)S(1)}, bf16[512,2048]{1,0:T(8,128)(2,1)S(1)}, bf16[512,2048]{1,0:T(8,128)(2,1)S(1)}, bf16[128,8192]{1,0:T(8,128)(2,1)S(1)}) custom-call(bf16[512,2048]{1,0:T(8,128)(2,1)} %q_h.1, bf16[512,2048]{1,0:T(8,128)(2,1)} %k_h.1, bf16[512,2048]{1,0:T(8,128)(2,1)} %v_h.1, bf16[128,8192]{1,0:T(8,128)(2,1)} %gate_h.1, ...), custom_call_target="tpu_custom_call" | custom-call | tf_op jit(solution)/shard_map/linear_attention_backward/pallas_call | solution.py:426
  77.1 3.4 %store_gradients.1 = (bf16[512,2048]{1,0:T(8,128)(2,1)}, bf16[512,2048]{1,0:T(8,128)(2,1)}, bf16[512,2048]{1,0:T(8,128)(2,1)}, bf16[128,8192]{1,0:T(8,128)(2,1)}) custom-call(bf16[512,2048]{1,0:T(8,128)(2,1)S(1)} %get-tuple-element.8.a, bf16[512,2048]{1,0:T(8,128)(2,1)S(1)} %get-tuple-element.9.b, bf16[512,2048]{1,0:T(8,128)(2,1)S(1)} %get-tuple-element.10.c, ...), custom_call_target="tpu_custom_call" | custom-call | tf_op jit(solution)/shard_map/store_gradients/pallas_call | solution.py:447

commit v3 on v2

--- a/solution.py
+++ b/solution.py
@@ -12,8 +12,8 @@
 MESH = pl.DeviceIdType.MESH
 F32 = jnp.float32
 BF16 = jnp.bfloat16
-FORWARD_LAG = 4
-BACKWARD_LAG = 2
+FORWARD_LAG = 3
+BACKWARD_LAG = 3
 
 
 def dot_nn(a, b):
@@ -64,7 +64,7 @@
     loads = [
         pltpu.make_async_copy(src, dst, in_sem.at[i])
         for i, (src, dst) in enumerate(
-            ((gain_h, gain), (gate_h, gate), (go_h, go), (k_h, k), (v_h, v), (q_h, q))
+            ((k_h, k), (v_h, v), (gain_h, gain), (gate_h, gate), (go_h, go), (q_h, q))
         )
     ]
     for load in loads:
@@ -169,13 +169,7 @@
             device_id={"seq": target}, device_id_type=MESH,
         )
 
-    for load in loads[:3]:
-        load.wait()
-    for d in order[:1]:
-        weigh(to_peer(d), False)
-        w_copy(d).start()
-
-    for load in loads[3:5]:
+    for load in loads[:2]:
         load.wait()
 
     def send_state(h, carry):
@@ -186,7 +180,9 @@
 
     lax.fori_loop(0, heads, send_state, 0)
 
-    for d in order[1:]:
+    for load in loads[2:5]:
+        load.wait()
+    for d in order:
         weigh(to_peer(d), False)
         w_copy(d).start()
     weigh(me, True)

time: 80.6 us -> 79.2 us (0.983)
  Pallas kernels: 79.8 us -> 78.4 us
    pallas_call x1, Pallas kernels: 76.4 us -> 75 us  [on_device(): pl.pallas_call(functools.partial(body, n_seq, n_head), out_shape=[wide, w...]
where the time goes in v3:
time: 79.2 us; the launch traced here: 79 us
  Pallas kernels  78.4 us (99%)
    pallas_call x1, Pallas kernels, on_device(): pl.pallas_call(functools.partial(body, n_seq, n_head), out_shape=[wide, w...  75 us
    pallas_call x1, Pallas kernels, on_device(): pl.pallas_call(store, out_shape=[jax.ShapeDtypeStruct(x.shape, BF16) for...  3.37 us

profile of v3, /device:TPU:0, one launch (start us, length us, event | category | flops | bytes accessed | tf_op | source)
XLA Modules:
  0.0 79.0 jit_solution(3104370361672134906)
XLA Ops:
  0.6 75.0 %linear_attention_backward.1 = (bf16[512,2048]{1,0:T(8,128)(2,1)S(1)}, bf16[512,2048]{1,0:T(8,128)(2,1)S(1)}, bf16[512,2048]{1,0:T(8,128)(2,1)S(1)}, bf16[128,8192]{1,0:T(8,128)(2,1)S(1)}) custom-call(bf16[512,2048]{1,0:T(8,128)(2,1)} %q_h.1, bf16[512,2048]{1,0:T(8,128)(2,1)} %k_h.1, bf16[512,2048]{1,0:T(8,128)(2,1)} %v_h.1, bf16[128,8192]{1,0:T(8,128)(2,1)} %gate_h.1, ...), custom_call_target="tpu_custom_call" | custom-call | tf_op jit(solution)/shard_map/linear_attention_backward/pallas_call | solution.py:422
  75.6 3.4 %store_gradients.1 = (bf16[512,2048]{1,0:T(8,128)(2,1)}, bf16[512,2048]{1,0:T(8,128)(2,1)}, bf16[512,2048]{1,0:T(8,128)(2,1)}, bf16[128,8192]{1,0:T(8,128)(2,1)}) custom-call(bf16[512,2048]{1,0:T(8,128)(2,1)S(1)} %get-tuple-element.8.a, bf16[512,2048]{1,0:T(8,128)(2,1)S(1)} %get-tuple-element.9.b, bf16[512,2048]{1,0:T(8,128)(2,1)S(1)} %get-tuple-element.10.c, ...), custom_call_target="tpu_custom_call" | custom-call | tf_op jit(solution)/shard_map/store_gradients/pallas_call | solution.py:443
